TPU v7x, 32 devices: a whole 2x2x4 slice. The times are simulated.
32 devices in a mesh: groups: 2 (over y), section: 2 (over x), band: 4 (over z), chan: 2 (over core).
Axes of the slice: x: 2, y: 2, z: 4, core: 2. Of those that a mesh axis runs over, the one named last changes fastest.
Arguments:
- latent: bfloat16 [16, 128, 640], P(('groups', 'band'), None, ('section', 'chan')), parts along dimension 0, may hold values from -6 to 6
- control_hint: bfloat16 [16, 128, 640], P(('groups', 'band'), None, ('section', 'chan')), parts along dimension 0, may hold values from -6 to 6
- control_weight_one: bfloat16 [3, 3, 640, 640], P(None, None, ('section', 'chan')), may hold values from -0.078125 to 0.078125
- control_bias_one: bfloat16 [640], P(('section', 'chan')), may hold values from -3 to 3
- control_weight_two: bfloat16 [3, 3, 640, 640], P(None, None, ('section', 'chan')), may hold values from -0.078125 to 0.078125
- control_bias_two: bfloat16 [640], P(('section', 'chan')), may hold values from -3 to 3
- main_weight_one: bfloat16 [3, 3, 640, 640], P(None, None, ('section', 'chan')), may hold values from -0.078125 to 0.078125
- main_bias_one: bfloat16 [640], P(('section', 'chan')), may hold values from -3 to 3
- main_weight_two: bfloat16 [3, 3, 640, 640], P(None, None, ('section', 'chan')), may hold values from -0.078125 to 0.078125
- main_bias_two: bfloat16 [640], P(('section', 'chan')), may hold values from -3 to 3
- decoder_weight_one: bfloat16 [3, 3, 640, 1280], P(None, None, ('section', 'chan')), may hold values from -0.0546875 to 0.0546875
- decoder_bias_one: bfloat16 [640], P(('section', 'chan')), may hold values from -3 to 3
- decoder_weight_two: bfloat16 [3, 3, 640, 1280], P(None, None, ('section', 'chan')), may hold values from -0.0546875 to 0.0546875
- decoder_bias_two: bfloat16 [640], P(('section', 'chan')), may hold values from -3 to 3
Outputs:
- decoded: bfloat16 [16, 128, 640], P(('groups', 'band'), None, ('section', 'chan')), parts along dimension 0
There are 2 independent parts, one for each index of `groups`. A program takes and returns all parts, laid end to end along the dimension named above; an argument that names none is the same for every part. Nothing has to cross between parts.
All inputs are finite; a program needn't handle non-finite values.
Results may differ from a plain program's by a relative error of at most 0.015.
Values may be sent and summed in bfloat16 or wider, within the bound.
No kernel may reach another device: no remote copies, remote signals or barrier semaphores. Data moves between devices by JAX's collectives and lax.ppermute only.
A program may use at most 64 MiB of HBM per device.

v0:
```python
import jax
import jax.numpy as jnp
from jax import lax
from jax.sharding import PartitionSpec as P

C = 640


def padded_2(cells, sides, width):
    for axis, dim in sides:
        count = lax.axis_size(axis)
        ends = count - 1
        head = lax.slice_in_dim(cells, 0, width, axis=dim)
        tail = lax.slice_in_dim(cells, cells.shape[dim] - width, cells.shape[dim], axis=dim)
        cells = jnp.concatenate(
            [
                lax.ppermute(tail, axis, [(i, (i + 1) % count) for i in range(ends)]),
                cells,
                lax.ppermute(head, axis, [((i + 1) % count, i) for i in range(ends)]),
            ],
            axis=dim,
        )
    return cells


def activate(state):
    value = state.astype(jnp.float32)
    return (value * jax.nn.sigmoid(value)).astype(jnp.bfloat16)


def add_taps(running, portion, anchor, weights):
    height = portion.shape[0] - 2
    breadth = portion.shape[1]
    depth = portion.shape[2]
    outputs = weights.shape[2]
    kernel = lax.dynamic_slice_in_dim(weights, anchor, depth, 3)
    kernel = jnp.transpose(kernel, (3, 0, 1, 2)).reshape(depth, 9 * outputs)
    product = jnp.dot(
        portion.reshape((height + 2) * breadth, depth), kernel, preferred_element_type=jnp.float32
    )
    product = product.reshape(height + 2, breadth, 9 * outputs)
    padded = jnp.pad(product, ((0, 0), (1, 1), (0, 0)))
    for row_step in range(3):
        for col_step in range(3):
            tap_index = row_step * 3 + col_step
            running = (
                running
                + padded[
                    row_step : row_step + height,
                    col_step : col_step + breadth,
                    tap_index * outputs : (tap_index + 1) * outputs,
                ]
            )
    return running


def convolve(activated, weights, skip_bordered):
    height, breadth = (activated.shape[0], activated.shape[1])
    outputs = weights.shape[2]
    empty = jnp.zeros((height, breadth, outputs), jnp.float32)
    bordered = padded_2(activated, (("band", 0),), 1)
    running = add_taps(
        empty,
        lax.all_gather(bordered, ("section", "chan"), axis=2, tiled=True),
        jnp.int32(0),
        weights,
    )
    if skip_bordered is not None:
        running = add_taps(running, skip_bordered, C, weights)
    return running


def residual_layer(state, weights, offset, skip_bordered):
    activated = activate(state)
    result = convolve(activated, weights, skip_bordered)
    total = state.astype(jnp.float32) + result + offset.astype(jnp.float32)
    return total.astype(jnp.bfloat16)


def per_device(
    latent,
    control_hint,
    control_weight_one,
    control_bias_one,
    control_weight_two,
    control_bias_two,
    main_weight_one,
    main_bias_one,
    main_weight_two,
    main_bias_two,
    decoder_weight_one,
    decoder_bias_one,
    decoder_weight_two,
    decoder_bias_two,
):
    control_input = (latent.astype(jnp.float32) + control_hint.astype(jnp.float32)).astype(
        jnp.bfloat16
    )
    control_mid = residual_layer(control_input, control_weight_one, control_bias_one, None)
    control_out = residual_layer(control_mid, control_weight_two, control_bias_two, None)
    main_mid = residual_layer(latent, main_weight_one, main_bias_one, None)
    main_out = residual_layer(main_mid, main_weight_two, main_bias_two, None)
    control_act = activate(control_out)
    skip_whole = lax.all_gather(control_act, ("section", "chan"), axis=2, tiled=True)
    skip_bordered = padded_2(skip_whole, (("band", 0),), 1)
    decoder_mid = residual_layer(main_out, decoder_weight_one, decoder_bias_one, skip_bordered)
    decoded = residual_layer(decoder_mid, decoder_weight_two, decoder_bias_two, skip_bordered)
    return decoded


def solution(mesh):
    placed = (
        P(("groups", "band"), None, ("section", "chan")),
        P(("groups", "band"), None, ("section", "chan")),
        P(None, None, ("section", "chan"), None),
        P(("section", "chan")),
        P(None, None, ("section", "chan"), None),
        P(("section", "chan")),
        P(None, None, ("section", "chan"), None),
        P(("section", "chan")),
        P(None, None, ("section", "chan"), None),
        P(("section", "chan")),
        P(None, None, ("section", "chan"), None),
        P(("section", "chan")),
        P(None, None, ("section", "chan"), None),
        P(("section", "chan")),
    )
    return jax.shard_map(
        per_device,
        mesh=mesh,
        in_specs=placed,
        out_specs=P(("groups", "band"), None, ("section", "chan")),
        check_vma=False,
    )
```

profile of v0, /device:TPU:0, one launch (start us, length us, event | category | flops | bytes accessed | tf_op | source)
XLA Modules:
  0.0 116.4 jit_solution(5973519125874029904)
XLA Ops:
  0.0 1.2 fusion.103
  1.2 5.0 %collective-permute-start = (bf16[1,128,160]{1,2,0:T(8,128)(2,1)S(1)}, bf16[1,128,160]{1,2,0:T(8,128)(2,1)S(1)}, u32[]{:S(2)}, u32[]{:S(2)}) collective-permute-start(bf16[1,128,160]{1,2,0:T(8,128)(2,1)S(1)} %get-tuple-element.27), channel_id=1, source_target_pairs={{0,2},{2,4},{4,6},{1,3},{3,5},{5,7},{8,10},{10,12},{12,14},{9,11},... | collective-permute-start | bytes 122888 | tf_op jit(solution)/shard_map/ppermute | solution.py:17
  6.1 1.3 %collective-permute-start.1 = (bf16[1,128,160]{1,2,0:T(8,128)(2,1)S(1)}, bf16[1,128,160]{1,2,0:T(8,128)(2,1)S(1)}, u32[]{:S(2)}, u32[]{:S(2)}) collective-permute-start(bf16[1,128,160]{1,2,0:T(8,128)(2,1)S(1)} %get-tuple-element.28), channel_id=1, source_target_pairs={{2,0},{4,2},{6,4},{3,1},{5,3},{7,5},{10,8},{12,10},{14,12},{11,9},... | collective-permute-start | bytes 122888 | tf_op jit(solution)/shard_map/ppermute | solution.py:19
  7.5 4.5 %collective-permute-start.6 = (bf16[1,128,160]{1,2,0:T(8,128)(2,1)S(1)}, bf16[1,128,160]{1,2,0:T(8,128)(2,1)S(1)}, u32[]{:S(2)}, u32[]{:S(2)}) collective-permute-start(bf16[1,128,160]{1,2,0:T(8,128)(2,1)S(1)} %get-tuple-element.33), channel_id=1, source_target_pairs={{0,2},{2,4},{4,6},{1,3},{3,5},{5,7},{8,10},{10,12},{12,14},{9,11},... | collective-permute-start | bytes 122888 | tf_op jit(solution)/shard_map/ppermute | solution.py:17
  12.0 0.0 copy-start.1
  12.0 1.6 %collective-permute-start.7 = (bf16[1,128,160]{1,2,0:T(8,128)(2,1)S(1)}, bf16[1,128,160]{1,2,0:T(8,128)(2,1)S(1)}, u32[]{:S(2)}, u32[]{:S(2)}) collective-permute-start(bf16[1,128,160]{1,2,0:T(8,128)(2,1)S(1)} %get-tuple-element.34), channel_id=1, source_target_pairs={{2,0},{4,2},{6,4},{3,1},{5,3},{7,5},{10,8},{12,10},{14,12},{11,9},... | collective-permute-start | bytes 122888 | tf_op jit(solution)/shard_map/ppermute | solution.py:19
  13.6 2.4 %fusion.112 = (bf16[3,3,160,640]{3,2,1,0:T(8,128)(2,1)S(1)}, bf16[3,3,160,640]{3,2,1,0:T(8,128)(2,1)S(1)}) fusion(bf16[3,3,160,1280]{3,2,1,0:T(8,128)(2,1)} %param.24), kind=kLoop, calls=%fused_computation.186 | loop fusion | bytes 7372800 | tf_op jit(solution)/shard_map/dynamic_slice | solution.py:36
  16.0 0.0 copy-start.7
  16.1 0.3 fusion.111
  16.4 0.3 copy-done.7
  16.7 0.0 copy-done.8
  16.7 0.0 copy-done.9
  16.7 0.0 copy-done.10
  16.7 0.0 copy-done.11
  16.7 0.0 copy-done.12
  16.7 1.4 %collective-permute-done.7 = bf16[1,128,160]{1,2,0:T(8,128)(2,1)S(1)} collective-permute-done((bf16[1,128,160]{1,2,0:T(8,128)(2,1)S(1)}, bf16[1,128,160]{1,2,0:T(8,128)(2,1)S(1)}, u32[]{:S(2)}, u32[]{:S(2)}) %collective-permute-start.7) | collective-permute-done | bytes 40992 | tf_op jit(solution)/shard_map/ppermute | solution.py:19
  18.2 7.9 %all_gather.24 = bf16[4,128,640]{1,2,0:T(8,128)(2,1)S(1)} all-gather(bf16[4,128,160]{1,2,0:T(8,128)(2,1)S(1)} %pad_maximum_fusion.3), channel_id=1, replica_groups=mesh['groups'=2,'section'=2,'band'=4,'chan'=2] {'section','chan'}, dimensions={2}, use_global_device_ids=true | all-gather | bytes 819200 | tf_op jit(solution)/shard_map/all_gather | solution.py:64
  26.1 8.0 %all_gather.21 = bf16[4,128,640]{1,2,0:T(8,128)(2,1)S(1)} all-gather(bf16[4,128,160]{1,2,0:T(8,128)(2,1)S(1)} %pad_maximum_fusion), channel_id=1, replica_groups=mesh['groups'=2,'section'=2,'band'=4,'chan'=2] {'section','chan'}, dimensions={2}, use_global_device_ids=true | all-gather | bytes 819200 | tf_op jit(solution)/shard_map/all_gather | solution.py:64
  34.1 1.3 %fusion.120 = f32[4,128,1440]{1,2,0:T(8,128)S(1)} fusion(bf16[640,1440,1]{0,1,2:T(8,128)(2,1)S(1)} %bitcast.56, bf16[4,128,640]{1,2,0:T(8,128)(2,1)S(1)} %all_gather.21), kind=kOutput, calls=%fused_computation.194 | convolution fusion | flops 943718400 | bytes 5447680 | tf_op jit(solution)/shard_map/dot_general | solution.py:38
  35.5 0.2 copy-done.4
  35.6 1.3 %fusion.123 = f32[4,128,1440]{1,2,0:T(8,128)S(1)} fusion(bf16[640,1440,1]{0,1,2:T(8,128)(2,1)S(1)} %bitcast.61, bf16[4,128,640]{1,2,0:T(8,128)(2,1)S(1)} %all_gather.24), kind=kOutput, calls=%fused_computation.197 | convolution fusion | flops 943718400 | bytes 5447680 | tf_op jit(solution)/shard_map/dot_general | solution.py:38
  37.0 0.6 fusion.73
  37.6 3.5 %collective-permute-start.8 = (bf16[1,128,160]{1,2,0:T(8,128)(2,1)S(1)}, bf16[1,128,160]{1,2,0:T(8,128)(2,1)S(1)}, u32[]{:S(2)}, u32[]{:S(2)}) collective-permute-start(bf16[1,128,160]{1,2,0:T(8,128)(2,1)S(1)} %get-tuple-element.31), channel_id=1, source_target_pairs={{0,2},{2,4},{4,6},{1,3},{3,5},{5,7},{8,10},{10,12},{12,14},{9,11},... | collective-permute-start | bytes 122888 | tf_op jit(solution)/shard_map/ppermute | solution.py:17
  41.1 1.3 %collective-permute-start.9 = (bf16[1,128,160]{1,2,0:T(8,128)(2,1)S(1)}, bf16[1,128,160]{1,2,0:T(8,128)(2,1)S(1)}, u32[]{:S(2)}, u32[]{:S(2)}) collective-permute-start(bf16[1,128,160]{1,2,0:T(8,128)(2,1)S(1)} %get-tuple-element.32), channel_id=1, source_target_pairs={{2,0},{4,2},{6,4},{3,1},{5,3},{7,5},{10,8},{12,10},{14,12},{11,9},... | collective-permute-start | bytes 122888 | tf_op jit(solution)/shard_map/ppermute | solution.py:19
  42.5 4.5 %collective-permute-start.2 = (bf16[1,128,160]{1,2,0:T(8,128)(2,1)S(1)}, bf16[1,128,160]{1,2,0:T(8,128)(2,1)S(1)}, u32[]{:S(2)}, u32[]{:S(2)}) collective-permute-start(bf16[1,128,160]{1,2,0:T(8,128)(2,1)S(1)} %get-tuple-element.23), channel_id=1, source_target_pairs={{0,2},{2,4},{4,6},{1,3},{3,5},{5,7},{8,10},{10,12},{12,14},{9,11},... | collective-permute-start | bytes 122888 | tf_op jit(solution)/shard_map/ppermute | solution.py:17
  47.0 1.3 %collective-permute-start.3 = (bf16[1,128,160]{1,2,0:T(8,128)(2,1)S(1)}, bf16[1,128,160]{1,2,0:T(8,128)(2,1)S(1)}, u32[]{:S(2)}, u32[]{:S(2)}) collective-permute-start(bf16[1,128,160]{1,2,0:T(8,128)(2,1)S(1)} %get-tuple-element.24), channel_id=1, source_target_pairs={{2,0},{4,2},{6,4},{3,1},{5,3},{7,5},{10,8},{12,10},{14,12},{11,9},... | collective-permute-start | bytes 122888 | tf_op jit(solution)/shard_map/ppermute | solution.py:19
  48.4 7.2 %all_gather.25 = bf16[4,128,640]{1,2,0:T(8,128)(2,1)S(1)} all-gather(bf16[4,128,160]{1,2,0:T(8,128)(2,1)S(1)} %pad_maximum_fusion.4), channel_id=1, replica_groups=mesh['groups'=2,'section'=2,'band'=4,'chan'=2] {'section','chan'}, dimensions={2}, use_global_device_ids=true | all-gather | bytes 819200 | tf_op jit(solution)/shard_map/all_gather | solution.py:64
  55.6 8.0 %all_gather.22 = bf16[4,128,640]{1,2,0:T(8,128)(2,1)S(1)} all-gather(bf16[4,128,160]{1,2,0:T(8,128)(2,1)S(1)} %pad_maximum_fusion.1), channel_id=1, replica_groups=mesh['groups'=2,'section'=2,'band'=4,'chan'=2] {'section','chan'}, dimensions={2}, use_global_device_ids=true | all-gather | bytes 819200 | tf_op jit(solution)/shard_map/all_gather | solution.py:64
  63.6 1.3 %fusion.121 = f32[4,128,1440]{1,2,0:T(8,128)S(1)} fusion(bf16[640,1440,1]{0,1,2:T(8,128)(2,1)S(1)} %bitcast.62, bf16[4,128,640]{1,2,0:T(8,128)(2,1)S(1)} %all_gather.22), kind=kOutput, calls=%fused_computation.195 | convolution fusion | flops 943718400 | bytes 5447680 | tf_op jit(solution)/shard_map/dot_general | solution.py:38
  64.9 0.4 fusion.79
  65.3 4.5 %collective-permute-start.4 = (bf16[1,128,160]{1,2,0:T(8,128)(2,1)S(1)}, bf16[1,128,160]{1,2,0:T(8,128)(2,1)S(1)}, u32[]{:S(2)}, u32[]{:S(2)}) collective-permute-start(bf16[1,128,160]{1,2,0:T(8,128)(2,1)S(1)} %get-tuple-element.21), channel_id=1, source_target_pairs={{0,2},{2,4},{4,6},{1,3},{3,5},{5,7},{8,10},{10,12},{12,14},{9,11},... | collective-permute-start | bytes 122888 | tf_op jit(solution)/shard_map/ppermute | solution.py:17
  69.7 1.3 %collective-permute-start.5 = (bf16[1,128,160]{1,2,0:T(8,128)(2,1)S(1)}, bf16[1,128,160]{1,2,0:T(8,128)(2,1)S(1)}, u32[]{:S(2)}, u32[]{:S(2)}) collective-permute-start(bf16[1,128,160]{1,2,0:T(8,128)(2,1)S(1)} %get-tuple-element.22), channel_id=1, source_target_pairs={{2,0},{4,2},{6,4},{3,1},{5,3},{7,5},{10,8},{12,10},{14,12},{11,9},... | collective-permute-start | bytes 122888 | tf_op jit(solution)/shard_map/ppermute | solution.py:19
  71.0 1.3 %fusion.124 = f32[4,128,1440]{1,2,0:T(8,128)S(1)} fusion(bf16[640,1440,1]{0,1,2:T(8,128)(2,1)S(1)} %bitcast.63, bf16[4,128,640]{1,2,0:T(8,128)(2,1)S(1)} %all_gather.25), kind=kOutput, calls=%fused_computation.198 | convolution fusion | flops 943718400 | bytes 5447680 | tf_op jit(solution)/shard_map/dot_general | solution.py:38
  72.4 0.4 fusion.69
  72.7 6.1 %all_gather.26 = bf16[2,128,640]{1,2,0:T(8,128)(2,1)S(1)} all-gather(bf16[2,128,160]{1,2,0:T(8,128)(2,1)S(1)} %fusion.69), channel_id=1, replica_groups=mesh['groups'=2,'section'=2,'band'=4,'chan'=2] {'section','chan'}, dimensions={2}, use_global_device_ids=true | all-gather | bytes 409600 | tf_op jit(solution)/shard_map/all_gather | solution.py:104
  78.9 1.3 %collective-permute-start.11 = (bf16[1,128,640]{1,2,0:T(8,128)(2,1)S(1)}, bf16[1,128,640]{1,2,0:T(8,128)(2,1)S(1)}, u32[]{:S(2)}, u32[]{:S(2)}) collective-permute-start(bf16[1,128,640]{1,2,0:T(8,128)(2,1)S(1)} %get-tuple-element.17), channel_id=1, source_target_pairs={{2,0},{4,2},{6,4},{3,1},{5,3},{7,5},{10,8},{12,10},{14,12},{11,9},... | collective-permute-start | bytes 491528 | tf_op jit(solution)/shard_map/ppermute | solution.py:19
  80.2 5.2 %collective-permute-start.10 = (bf16[1,128,640]{1,2,0:T(8,128)(2,1)S(1)}, bf16[1,128,640]{1,2,0:T(8,128)(2,1)S(1)}, u32[]{:S(2)}, u32[]{:S(2)}) collective-permute-start(bf16[1,128,640]{1,2,0:T(8,128)(2,1)S(1)} %get-tuple-element.18), channel_id=1, source_target_pairs={{0,2},{2,4},{4,6},{1,3},{3,5},{5,7},{8,10},{10,12},{12,14},{9,11},... | collective-permute-start | bytes 491528 | tf_op jit(solution)/shard_map/ppermute | solution.py:17
  85.4 7.7 %all_gather.23 = bf16[4,128,640]{1,2,0:T(8,128)(2,1)S(1)} all-gather(bf16[4,128,160]{1,2,0:T(8,128)(2,1)S(1)} %pad_maximum_fusion.2), channel_id=1, replica_groups=mesh['groups'=2,'section'=2,'band'=4,'chan'=2] {'section','chan'}, dimensions={2}, use_global_device_ids=true | all-gather | bytes 819200 | tf_op jit(solution)/shard_map/all_gather | solution.py:64
  93.1 1.3 %fusion.122 = f32[4,128,1440]{1,2,0:T(8,128)S(1)} fusion(bf16[640,1440,1]{0,1,2:T(8,128)(2,1)S(1)} %bitcast.60, bf16[4,128,640]{1,2,0:T(8,128)(2,1)S(1)} %all_gather.23), kind=kOutput, calls=%fused_computation.196 | convolution fusion | flops 943718400 | bytes 5447680 | tf_op jit(solution)/shard_map/dot_general | solution.py:38
  94.6 1.3 %fusion.125 = f32[4,128,1440]{1,2,0:T(8,128)S(1)} fusion(bf16[640,1440,1]{0,1,2:T(8,128)(2,1)S(1)} %bitcast.59, bf16[4,128,640]{1,2,0:T(8,128)(2,1)S(1)} %constant_dynamic-update-slice_fusion), kind=kOutput, calls=%fused_computation.199 | convolution fusion | flops 943718400 | bytes 5447680 | tf_op jit(solution)/shard_map/dot_general | solution.py:38
  95.9 0.6 fusion.97
  96.6 3.9 %collective-permute-start.12 = (bf16[1,128,160]{1,2,0:T(8,128)(2,1)S(1)}, bf16[1,128,160]{1,2,0:T(8,128)(2,1)S(1)}, u32[]{:S(2)}, u32[]{:S(2)}) collective-permute-start(bf16[1,128,160]{1,2,0:T(8,128)(2,1)S(1)} %get-tuple-element.19), channel_id=1, source_target_pairs={{0,2},{2,4},{4,6},{1,3},{3,5},{5,7},{8,10},{10,12},{12,14},{9,11},... | collective-permute-start | bytes 122888 | tf_op jit(solution)/shard_map/ppermute | solution.py:17
  100.5 1.5 %collective-permute-start.13 = (bf16[1,128,160]{1,2,0:T(8,128)(2,1)S(1)}, bf16[1,128,160]{1,2,0:T(8,128)(2,1)S(1)}, u32[]{:S(2)}, u32[]{:S(2)}) collective-permute-start(bf16[1,128,160]{1,2,0:T(8,128)(2,1)S(1)} %get-tuple-element.20), channel_id=1, source_target_pairs={{2,0},{4,2},{6,4},{3,1},{5,3},{7,5},{10,8},{12,10},{14,12},{11,9},... | collective-permute-start | bytes 122888 | tf_op jit(solution)/shard_map/ppermute | solution.py:19
  102.0 1.3 %fusion.127 = f32[4,128,1440]{1,2,0:T(8,128)S(1)} fusion(bf16[640,1440,1]{0,1,2:T(8,128)(2,1)S(1)} %bitcast.58, bf16[4,128,640]{1,2,0:T(8,128)(2,1)S(1)} %constant_dynamic-update-slice_fusion), kind=kOutput, calls=%fused_computation.201 | convolution fusion | flops 943718400 | bytes 5447680 | tf_op jit(solution)/shard_map/dot_general | solution.py:38
  103.3 3.1 %collective-permute-done.13 = bf16[1,128,160]{1,2,0:T(8,128)(2,1)S(1)} collective-permute-done((bf16[1,128,160]{1,2,0:T(8,128)(2,1)S(1)}, bf16[1,128,160]{1,2,0:T(8,128)(2,1)S(1)}, u32[]{:S(2)}, u32[]{:S(2)}) %collective-permute-start.13) | collective-permute-done | bytes 40992 | tf_op jit(solution)/shard_map/ppermute | solution.py:19
  106.4 7.4 %all_gather.27 = bf16[4,128,640]{1,2,0:T(8,128)(2,1)S(1)} all-gather(bf16[4,128,160]{1,2,0:T(8,128)(2,1)S(1)} %pad_maximum_fusion.5), channel_id=1, replica_groups=mesh['groups'=2,'section'=2,'band'=4,'chan'=2] {'section','chan'}, dimensions={2}, use_global_device_ids=true | all-gather | bytes 819200 | tf_op jit(solution)/shard_map/all_gather | solution.py:64
  113.8 1.3 %fusion.126 = f32[4,128,1440]{1,2,0:T(8,128)S(1)} fusion(bf16[640,1440,1]{0,1,2:T(8,128)(2,1)S(1)} %bitcast.57, bf16[4,128,640]{1,2,0:T(8,128)(2,1)S(1)} %all_gather.27), kind=kOutput, calls=%fused_computation.200 | convolution fusion | flops 943718400 | bytes 5447680 | tf_op jit(solution)/shard_map/dot_general | solution.py:38
  115.1 1.2 %fusion.99 = bf16[2,128,160]{1,2,0:T(8,128)(2,1)} fusion(bf16[2,128,160]{1,2,0:T(8,128)(2,1)S(1)} %get-tuple-element.6, f32[4,128,1440]{1,2,0:T(8,128)S(1)} %fusion.127, f32[4,128,1440]{1,2,0:T(8,128)S(1)} %fusion.126, f32[160]{0:T(256)S(1)} %convert_element_type.126), kind=kLoop, calls=%fused_computation.168 | loop fusion | flops 860160 | bytes 7046144 | tf_op jit(solution)/shard_map/convert_element_type | solution.py:77
  (51 shorter events, 0.4 us)
Async XLA Ops:
  0.0 34.1 %copy-start = (bf16[3,3,160,640]{3,2,1,0:T(8,128)(2,1)S(1)}, bf16[3,3,160,640]{3,2,1,0:T(8,128)(2,1)}, u32[]{:S(2)}) copy-start(bf16[3,3,160,640]{3,2,1,0:T(8,128)(2,1)} %param.20) | copy-start | bytes 5529604
  1.2 24.9 %collective-permute-start = (bf16[1,128,160]{1,2,0:T(8,128)(2,1)S(1)}, bf16[1,128,160]{1,2,0:T(8,128)(2,1)S(1)}, u32[]{:S(2)}, u32[]{:S(2)}) collective-permute-start(bf16[1,128,160]{1,2,0:T(8,128)(2,1)S(1)} %get-tuple-element.27), channel_id=1, source_target_pairs={{0,2},{2,4},{4,6},{1,3},{3,5},{5,7},{8,10},{10,12},{12,14},{9,11},... | collective-permute-start | bytes 122888 | tf_op jit(solution)/shard_map/ppermute | solution.py:17
  6.1 20.0 %collective-permute-start.1 = (bf16[1,128,160]{1,2,0:T(8,128)(2,1)S(1)}, bf16[1,128,160]{1,2,0:T(8,128)(2,1)S(1)}, u32[]{:S(2)}, u32[]{:S(2)}) collective-permute-start(bf16[1,128,160]{1,2,0:T(8,128)(2,1)S(1)} %get-tuple-element.28), channel_id=1, source_target_pairs={{2,0},{4,2},{6,4},{3,1},{5,3},{7,5},{10,8},{12,10},{14,12},{11,9},... | collective-permute-start | bytes 122888 | tf_op jit(solution)/shard_map/ppermute | solution.py:19
  7.5 9.3 %collective-permute-start.6 = (bf16[1,128,160]{1,2,0:T(8,128)(2,1)S(1)}, bf16[1,128,160]{1,2,0:T(8,128)(2,1)S(1)}, u32[]{:S(2)}, u32[]{:S(2)}) collective-permute-start(bf16[1,128,160]{1,2,0:T(8,128)(2,1)S(1)} %get-tuple-element.33), channel_id=1, source_target_pairs={{0,2},{2,4},{4,6},{1,3},{3,5},{5,7},{8,10},{10,12},{12,14},{9,11},... | collective-permute-start | bytes 122888 | tf_op jit(solution)/shard_map/ppermute | solution.py:17
  12.0 4.0 %copy-start.1 = (bf16[3,3,160,1280]{3,2,1,0:T(8,128)(2,1)S(1)}, bf16[3,3,160,1280]{3,2,1,0:T(8,128)(2,1)}, u32[]{:S(2)}) copy-start(bf16[3,3,160,1280]{3,2,1,0:T(8,128)(2,1)} %param.26) | copy-start | bytes 11059204
  12.0 6.2 %collective-permute-start.7 = (bf16[1,128,160]{1,2,0:T(8,128)(2,1)S(1)}, bf16[1,128,160]{1,2,0:T(8,128)(2,1)S(1)}, u32[]{:S(2)}, u32[]{:S(2)}) collective-permute-start(bf16[1,128,160]{1,2,0:T(8,128)(2,1)S(1)} %get-tuple-element.34), channel_id=1, source_target_pairs={{2,0},{4,2},{6,4},{3,1},{5,3},{7,5},{10,8},{12,10},{14,12},{11,9},... | collective-permute-start | bytes 122888 | tf_op jit(solution)/shard_map/ppermute | solution.py:19
  16.0 0.7 copy-start.7
  16.0 0.7 copy-start.8
  16.0 0.7 copy-start.9
  16.0 0.7 copy-start.10
  16.0 0.7 copy-start.11
  16.0 0.7 copy-start.12
  34.1 1.5 %copy-start.4 = (bf16[3,3,160,640]{3,2,1,0:T(8,128)(2,1)S(1)}, bf16[3,3,160,640]{3,2,1,0:T(8,128)(2,1)}, u32[]{:S(2)}) copy-start(bf16[3,3,160,640]{3,2,1,0:T(8,128)(2,1)} %param.16) | copy-start | bytes 5529604
  35.4 1.5 %copy-start.2 = (bf16[2,128,160]{1,2,0:T(8,128)(2,1)S(1)}, bf16[2,128,160]{1,2,0:T(8,128)(2,1)}, u32[]{:S(2)}) copy-start(bf16[2,128,160]{1,2,0:T(8,128)(2,1)} %param.14) | copy-start | bytes 245764
  35.5 1.5 %copy-start.3 = (bf16[2,128,160]{1,2,0:T(8,128)(2,1)S(1)}, bf16[2,128,160]{1,2,0:T(8,128)(2,1)}, u32[]{:S(2)}) copy-start(bf16[2,128,160]{1,2,0:T(8,128)(2,1)} %param.15) | copy-start | bytes 245764
  37.0 26.6 %copy-start.5 = (bf16[3,3,160,640]{3,2,1,0:T(8,128)(2,1)S(1)}, bf16[3,3,160,640]{3,2,1,0:T(8,128)(2,1)}, u32[]{:S(2)}) copy-start(bf16[3,3,160,640]{3,2,1,0:T(8,128)(2,1)} %param.22) | copy-start | bytes 5529604
  37.6 10.7 %collective-permute-start.8 = (bf16[1,128,160]{1,2,0:T(8,128)(2,1)S(1)}, bf16[1,128,160]{1,2,0:T(8,128)(2,1)S(1)}, u32[]{:S(2)}, u32[]{:S(2)}) collective-permute-start(bf16[1,128,160]{1,2,0:T(8,128)(2,1)S(1)} %get-tuple-element.31), channel_id=1, source_target_pairs={{0,2},{2,4},{4,6},{1,3},{3,5},{5,7},{8,10},{10,12},{12,14},{9,11},... | collective-permute-start | bytes 122888 | tf_op jit(solution)/shard_map/ppermute | solution.py:17
  41.1 7.2 %collective-permute-start.9 = (bf16[1,128,160]{1,2,0:T(8,128)(2,1)S(1)}, bf16[1,128,160]{1,2,0:T(8,128)(2,1)S(1)}, u32[]{:S(2)}, u32[]{:S(2)}) collective-permute-start(bf16[1,128,160]{1,2,0:T(8,128)(2,1)S(1)} %get-tuple-element.32), channel_id=1, source_target_pairs={{2,0},{4,2},{6,4},{3,1},{5,3},{7,5},{10,8},{12,10},{14,12},{11,9},... | collective-permute-start | bytes 122888 | tf_op jit(solution)/shard_map/ppermute | solution.py:19
  42.5 13.1 %collective-permute-start.2 = (bf16[1,128,160]{1,2,0:T(8,128)(2,1)S(1)}, bf16[1,128,160]{1,2,0:T(8,128)(2,1)S(1)}, u32[]{:S(2)}, u32[]{:S(2)}) collective-permute-start(bf16[1,128,160]{1,2,0:T(8,128)(2,1)S(1)} %get-tuple-element.23), channel_id=1, source_target_pairs={{0,2},{2,4},{4,6},{1,3},{3,5},{5,7},{8,10},{10,12},{12,14},{9,11},... | collective-permute-start | bytes 122888 | tf_op jit(solution)/shard_map/ppermute | solution.py:17
  47.0 8.5 %collective-permute-start.3 = (bf16[1,128,160]{1,2,0:T(8,128)(2,1)S(1)}, bf16[1,128,160]{1,2,0:T(8,128)(2,1)S(1)}, u32[]{:S(2)}, u32[]{:S(2)}) collective-permute-start(bf16[1,128,160]{1,2,0:T(8,128)(2,1)S(1)} %get-tuple-element.24), channel_id=1, source_target_pairs={{2,0},{4,2},{6,4},{3,1},{5,3},{7,5},{10,8},{12,10},{14,12},{11,9},... | collective-permute-start | bytes 122888 | tf_op jit(solution)/shard_map/ppermute | solution.py:19
  64.9 6.2 %copy-start.6 = (bf16[3,3,160,640]{3,2,1,0:T(8,128)(2,1)S(1)}, bf16[3,3,160,640]{3,2,1,0:T(8,128)(2,1)}, u32[]{:S(2)}) copy-start(bf16[3,3,160,640]{3,2,1,0:T(8,128)(2,1)} %param.18) | copy-start | bytes 5529604
  65.3 20.1 %collective-permute-start.4 = (bf16[1,128,160]{1,2,0:T(8,128)(2,1)S(1)}, bf16[1,128,160]{1,2,0:T(8,128)(2,1)S(1)}, u32[]{:S(2)}, u32[]{:S(2)}) collective-permute-start(bf16[1,128,160]{1,2,0:T(8,128)(2,1)S(1)} %get-tuple-element.21), channel_id=1, source_target_pairs={{0,2},{2,4},{4,6},{1,3},{3,5},{5,7},{8,10},{10,12},{12,14},{9,11},... | collective-permute-start | bytes 122888 | tf_op jit(solution)/shard_map/ppermute | solution.py:17
  69.7 15.6 %collective-permute-start.5 = (bf16[1,128,160]{1,2,0:T(8,128)(2,1)S(1)}, bf16[1,128,160]{1,2,0:T(8,128)(2,1)S(1)}, u32[]{:S(2)}, u32[]{:S(2)}) collective-permute-start(bf16[1,128,160]{1,2,0:T(8,128)(2,1)S(1)} %get-tuple-element.22), channel_id=1, source_target_pairs={{2,0},{4,2},{6,4},{3,1},{5,3},{7,5},{10,8},{12,10},{14,12},{11,9},... | collective-permute-start | bytes 122888 | tf_op jit(solution)/shard_map/ppermute | solution.py:19
  78.9 15.7 %collective-permute-start.11 = (bf16[1,128,640]{1,2,0:T(8,128)(2,1)S(1)}, bf16[1,128,640]{1,2,0:T(8,128)(2,1)S(1)}, u32[]{:S(2)}, u32[]{:S(2)}) collective-permute-start(bf16[1,128,640]{1,2,0:T(8,128)(2,1)S(1)} %get-tuple-element.17), channel_id=1, source_target_pairs={{2,0},{4,2},{6,4},{3,1},{5,3},{7,5},{10,8},{12,10},{14,12},{11,9},... | collective-permute-start | bytes 491528 | tf_op jit(solution)/shard_map/ppermute | solution.py:19
  80.2 14.3 %collective-permute-start.10 = (bf16[1,128,640]{1,2,0:T(8,128)(2,1)S(1)}, bf16[1,128,640]{1,2,0:T(8,128)(2,1)S(1)}, u32[]{:S(2)}, u32[]{:S(2)}) collective-permute-start(bf16[1,128,640]{1,2,0:T(8,128)(2,1)S(1)} %get-tuple-element.18), channel_id=1, source_target_pairs={{0,2},{2,4},{4,6},{1,3},{3,5},{5,7},{8,10},{10,12},{12,14},{9,11},... | collective-permute-start | bytes 491528 | tf_op jit(solution)/shard_map/ppermute | solution.py:17
  96.6 6.7 %collective-permute-start.12 = (bf16[1,128,160]{1,2,0:T(8,128)(2,1)S(1)}, bf16[1,128,160]{1,2,0:T(8,128)(2,1)S(1)}, u32[]{:S(2)}, u32[]{:S(2)}) collective-permute-start(bf16[1,128,160]{1,2,0:T(8,128)(2,1)S(1)} %get-tuple-element.19), channel_id=1, source_target_pairs={{0,2},{2,4},{4,6},{1,3},{3,5},{5,7},{8,10},{10,12},{12,14},{9,11},... | collective-permute-start | bytes 122888 | tf_op jit(solution)/shard_map/ppermute | solution.py:17
  100.5 5.9 %collective-permute-start.13 = (bf16[1,128,160]{1,2,0:T(8,128)(2,1)S(1)}, bf16[1,128,160]{1,2,0:T(8,128)(2,1)S(1)}, u32[]{:S(2)}, u32[]{:S(2)}) collective-permute-start(bf16[1,128,160]{1,2,0:T(8,128)(2,1)S(1)} %get-tuple-element.20), channel_id=1, source_target_pairs={{2,0},{4,2},{6,4},{3,1},{5,3},{7,5},{10,8},{12,10},{14,12},{11,9},... | collective-permute-start | bytes 122888 | tf_op jit(solution)/shard_map/ppermute | solution.py:19
where the time goes:
time: 117 us; the launch traced here: 116 us
  blocking collectives  52.3 us (45%)
  starting transfers between devices  40.6 us (35%)
  matrix products  10.5 us (9%)
  waiting for transfers between devices  4.56 us (4%)
  other arithmetic  4.51 us (4%)
  local copies, waits for them, and re-layouts  3.39 us (3%)
    all_gather x6, blocking collectives, convolve(): lax.all_gather(bordered, ('section', 'chan'), axis=2, tiled=True)  46.2 us
    ppermute x7, starting transfers between devices, padded_2(): lax.ppermute(tail, axis, [(i, (i + 1) % count) for i in range(ends)])  31.1 us
    dot_general x8, matrix products, add_taps(): jnp.dot(portion.reshape((height + 2) * breadth, depth), kernel, preferred...  10.5 us
    ppermute x7, starting transfers between devices, padded_2(): lax.ppermute(head, axis, [((i + 1) % count, i) for i in range(ends)])  9.49 us
    all_gather x1, blocking collectives, per_device(): lax.all_gather(control_act, ('section', 'chan'), axis=2, tiled=True)  6.1 us
    ppermute x7, waiting for transfers between devices, padded_2(): lax.ppermute(head, axis, [((i + 1) % count, i) for i in range(ends)])  4.54 us
    convert_element_type x5, other arithmetic, activate(): return (value * jax.nn.sigmoid(value)).astype(jnp.bfloat16)  3.12 us
    dynamic_slice x2, local copies, waits for them, and re-layouts, add_taps(): kernel = lax.dynamic_slice_in_dim(weights, anchor, depth, 3)  2.7 us
  transfers between devices with their start and end apart: 14, of which 2 were waited for; matrix products, arithmetic and copies ran while one was open for 6% of the time, Pallas kernels for 0%

commit v1 on v0

--- a/solution.py
+++ b/solution.py
@@ -61,7 +61,7 @@
     bordered = padded_2(activated, (("band", 0),), 1)
     running = add_taps(
         empty,
-        lax.all_gather(bordered, ("section", "chan"), axis=2, tiled=True),
+        jnp.concatenate(lax.all_gather(bordered, ("section", "chan")), axis=2),
         jnp.int32(0),
         weights,
     )

time: 117 us -> 118 us (level)
  no operation moved by 1% of the time
where the time goes in v1:
time: 118 us; the launch traced here: 117 us
  blocking collectives  52.3 us (44%)
  starting transfers between devices  40.7 us (34%)
  matrix products  10.5 us (9%)
  waiting for transfers between devices  4.74 us (4%)
  other arithmetic  4.51 us (4%)
  local copies, waits for them, and re-layouts  3.64 us (3%)
    all_gather x6, blocking collectives, convolve(): lax.all_gather(bordered, ('section', 'chan'))  46.2 us
    ppermute x7, starting transfers between devices, padded_2(): lax.ppermute(tail, axis, [(i, (i + 1) % count) for i in range(ends)])  31.2 us
    dot_general x8, matrix products, add_taps(): jnp.dot(portion.reshape((height + 2) * breadth, depth), kernel, preferred...  10.5 us
    ppermute x7, starting transfers between devices, padded_2(): lax.ppermute(head, axis, [((i + 1) % count, i) for i in range(ends)])  9.49 us
    all_gather x1, blocking collectives, per_device(): lax.all_gather(control_act, ('section', 'chan'), axis=2, tiled=True)  6.1 us
    ppermute x7, waiting for transfers between devices, padded_2(): lax.ppermute(head, axis, [((i + 1) % count, i) for i in range(ends)])  4.72 us
    convert_element_type x5, other arithmetic, activate(): return (value * jax.nn.sigmoid(value)).astype(jnp.bfloat16)  3.12 us
    dynamic_slice x2, local copies, waits for them, and re-layouts, add_taps(): kernel = lax.dynamic_slice_in_dim(weights, anchor, depth, 3)  2.7 us
  transfers between devices with their start and end apart: 14, of which 2 were waited for; matrix products, arithmetic and copies ran while one was open for 6% of the time, Pallas kernels for 0%

profile of v1, /device:TPU:0, one launch (start us, length us, event | category | flops | bytes accessed | tf_op | source)
XLA Modules:
  0.0 117.0 jit_solution(10713641388621007541)
XLA Ops:
  0.0 1.2 fusion.103
  1.2 5.0 %collective-permute-start = (bf16[1,128,160]{1,2,0:T(8,128)(2,1)S(1)}, bf16[1,128,160]{1,2,0:T(8,128)(2,1)S(1)}, u32[]{:S(2)}, u32[]{:S(2)}) collective-permute-start(bf16[1,128,160]{1,2,0:T(8,128)(2,1)S(1)} %get-tuple-element.27), channel_id=1, source_target_pairs={{0,2},{2,4},{4,6},{1,3},{3,5},{5,7},{8,10},{10,12},{12,14},{9,11},... | collective-permute-start | bytes 122888 | tf_op jit(solution)/shard_map/ppermute | solution.py:17
  6.1 1.3 %collective-permute-start.1 = (bf16[1,128,160]{1,2,0:T(8,128)(2,1)S(1)}, bf16[1,128,160]{1,2,0:T(8,128)(2,1)S(1)}, u32[]{:S(2)}, u32[]{:S(2)}) collective-permute-start(bf16[1,128,160]{1,2,0:T(8,128)(2,1)S(1)} %get-tuple-element.28), channel_id=1, source_target_pairs={{2,0},{4,2},{6,4},{3,1},{5,3},{7,5},{10,8},{12,10},{14,12},{11,9},... | collective-permute-start | bytes 122888 | tf_op jit(solution)/shard_map/ppermute | solution.py:19
  7.5 4.5 %collective-permute-start.6 = (bf16[1,128,160]{1,2,0:T(8,128)(2,1)S(1)}, bf16[1,128,160]{1,2,0:T(8,128)(2,1)S(1)}, u32[]{:S(2)}, u32[]{:S(2)}) collective-permute-start(bf16[1,128,160]{1,2,0:T(8,128)(2,1)S(1)} %get-tuple-element.33), channel_id=1, source_target_pairs={{0,2},{2,4},{4,6},{1,3},{3,5},{5,7},{8,10},{10,12},{12,14},{9,11},... | collective-permute-start | bytes 122888 | tf_op jit(solution)/shard_map/ppermute | solution.py:17
  12.0 0.0 copy-start.1
  12.0 1.6 %collective-permute-start.7 = (bf16[1,128,160]{1,2,0:T(8,128)(2,1)S(1)}, bf16[1,128,160]{1,2,0:T(8,128)(2,1)S(1)}, u32[]{:S(2)}, u32[]{:S(2)}) collective-permute-start(bf16[1,128,160]{1,2,0:T(8,128)(2,1)S(1)} %get-tuple-element.34), channel_id=1, source_target_pairs={{2,0},{4,2},{6,4},{3,1},{5,3},{7,5},{10,8},{12,10},{14,12},{11,9},... | collective-permute-start | bytes 122888 | tf_op jit(solution)/shard_map/ppermute | solution.py:19
  13.6 2.4 %fusion.112 = (bf16[3,3,160,640]{3,2,1,0:T(8,128)(2,1)S(1)}, bf16[3,3,160,640]{3,2,1,0:T(8,128)(2,1)S(1)}) fusion(bf16[3,3,160,1280]{3,2,1,0:T(8,128)(2,1)} %param.24), kind=kLoop, calls=%fused_computation.186 | loop fusion | bytes 7372800 | tf_op jit(solution)/shard_map/dynamic_slice | solution.py:36
  16.0 0.0 copy-start.7
  16.1 0.3 fusion.111
  16.4 0.3 copy-done.7
  16.7 0.0 copy-done.8
  16.7 0.0 copy-done.9
  16.7 0.0 copy-done.10
  16.7 0.0 copy-done.11
  16.7 0.0 copy-done.12
  16.7 1.4 %collective-permute-done.7 = bf16[1,128,160]{1,2,0:T(8,128)(2,1)S(1)} collective-permute-done((bf16[1,128,160]{1,2,0:T(8,128)(2,1)S(1)}, bf16[1,128,160]{1,2,0:T(8,128)(2,1)S(1)}, u32[]{:S(2)}, u32[]{:S(2)}) %collective-permute-start.7) | collective-permute-done | bytes 40992 | tf_op jit(solution)/shard_map/ppermute | solution.py:19
  18.2 7.9 %all-gather.3 = bf16[16,128,160]{1,2,0:T(8,128)(2,1)S(1)} all-gather(bf16[4,128,160]{1,2,0:T(8,128)(2,1)S(1)} %pad_maximum_fusion.3), channel_id=5, replica_groups=mesh['groups'=2,'section'=2,'band'=4,'chan'=2] {'section','chan'}, dimensions={0}, use_global_device_ids=true | all-gather | bytes 819200 | tf_op jit(solution)/shard_map/all_gather | solution.py:64
  26.2 8.0 %all-gather = bf16[16,128,160]{1,2,0:T(8,128)(2,1)S(1)} all-gather(bf16[4,128,160]{1,2,0:T(8,128)(2,1)S(1)} %pad_maximum_fusion), channel_id=2, replica_groups=mesh['groups'=2,'section'=2,'band'=4,'chan'=2] {'section','chan'}, dimensions={0}, use_global_device_ids=true | all-gather | bytes 819200 | tf_op jit(solution)/shard_map/all_gather | solution.py:64
  34.3 1.3 %fusion.120 = f32[4,128,1440]{1,2,0:T(8,128)S(1)} fusion(bf16[640,1440,1]{0,1,2:T(8,128)(2,1)S(1)} %bitcast.80, bf16[4,128,640]{1,2,0:T(8,128)(2,1)S(1)} %bitcast.95), kind=kOutput, calls=%fused_computation.194 | convolution fusion | flops 943718400 | bytes 5447680 | tf_op jit(solution)/shard_map/dot_general | solution.py:38
  35.6 0.2 copy-done.4
  35.8 1.3 %fusion.123 = f32[4,128,1440]{1,2,0:T(8,128)S(1)} fusion(bf16[640,1440,1]{0,1,2:T(8,128)(2,1)S(1)} %bitcast.97, bf16[4,128,640]{1,2,0:T(8,128)(2,1)S(1)} %bitcast.92), kind=kOutput, calls=%fused_computation.197 | convolution fusion | flops 943718400 | bytes 5447680 | tf_op jit(solution)/shard_map/dot_general | solution.py:38
  37.1 0.6 fusion.73
  37.8 3.6 %collective-permute-start.8 = (bf16[1,128,160]{1,2,0:T(8,128)(2,1)S(1)}, bf16[1,128,160]{1,2,0:T(8,128)(2,1)S(1)}, u32[]{:S(2)}, u32[]{:S(2)}) collective-permute-start(bf16[1,128,160]{1,2,0:T(8,128)(2,1)S(1)} %get-tuple-element.31), channel_id=1, source_target_pairs={{0,2},{2,4},{4,6},{1,3},{3,5},{5,7},{8,10},{10,12},{12,14},{9,11},... | collective-permute-start | bytes 122888 | tf_op jit(solution)/shard_map/ppermute | solution.py:17
  41.4 1.3 %collective-permute-start.9 = (bf16[1,128,160]{1,2,0:T(8,128)(2,1)S(1)}, bf16[1,128,160]{1,2,0:T(8,128)(2,1)S(1)}, u32[]{:S(2)}, u32[]{:S(2)}) collective-permute-start(bf16[1,128,160]{1,2,0:T(8,128)(2,1)S(1)} %get-tuple-element.32), channel_id=1, source_target_pairs={{2,0},{4,2},{6,4},{3,1},{5,3},{7,5},{10,8},{12,10},{14,12},{11,9},... | collective-permute-start | bytes 122888 | tf_op jit(solution)/shard_map/ppermute | solution.py:19
  42.7 4.5 %collective-permute-start.2 = (bf16[1,128,160]{1,2,0:T(8,128)(2,1)S(1)}, bf16[1,128,160]{1,2,0:T(8,128)(2,1)S(1)}, u32[]{:S(2)}, u32[]{:S(2)}) collective-permute-start(bf16[1,128,160]{1,2,0:T(8,128)(2,1)S(1)} %get-tuple-element.23), channel_id=1, source_target_pairs={{0,2},{2,4},{4,6},{1,3},{3,5},{5,7},{8,10},{10,12},{12,14},{9,11},... | collective-permute-start | bytes 122888 | tf_op jit(solution)/shard_map/ppermute | solution.py:17
  47.3 1.3 %collective-permute-start.3 = (bf16[1,128,160]{1,2,0:T(8,128)(2,1)S(1)}, bf16[1,128,160]{1,2,0:T(8,128)(2,1)S(1)}, u32[]{:S(2)}, u32[]{:S(2)}) collective-permute-start(bf16[1,128,160]{1,2,0:T(8,128)(2,1)S(1)} %get-tuple-element.24), channel_id=1, source_target_pairs={{2,0},{4,2},{6,4},{3,1},{5,3},{7,5},{10,8},{12,10},{14,12},{11,9},... | collective-permute-start | bytes 122888 | tf_op jit(solution)/shard_map/ppermute | solution.py:19
  48.6 7.2 %all-gather.4 = bf16[16,128,160]{1,2,0:T(8,128)(2,1)S(1)} all-gather(bf16[4,128,160]{1,2,0:T(8,128)(2,1)S(1)} %pad_maximum_fusion.4), channel_id=6, replica_groups=mesh['groups'=2,'section'=2,'band'=4,'chan'=2] {'section','chan'}, dimensions={0}, use_global_device_ids=true | all-gather | bytes 819200 | tf_op jit(solution)/shard_map/all_gather | solution.py:64
  55.9 8.0 %all-gather.1 = bf16[16,128,160]{1,2,0:T(8,128)(2,1)S(1)} all-gather(bf16[4,128,160]{1,2,0:T(8,128)(2,1)S(1)} %pad_maximum_fusion.1), channel_id=3, replica_groups=mesh['groups'=2,'section'=2,'band'=4,'chan'=2] {'section','chan'}, dimensions={0}, use_global_device_ids=true | all-gather | bytes 819200 | tf_op jit(solution)/shard_map/all_gather | solution.py:64
  63.9 1.3 %fusion.121 = f32[4,128,1440]{1,2,0:T(8,128)S(1)} fusion(bf16[640,1440,1]{0,1,2:T(8,128)(2,1)S(1)} %bitcast.98, bf16[4,128,640]{1,2,0:T(8,128)(2,1)S(1)} %bitcast.96), kind=kOutput, calls=%fused_computation.195 | convolution fusion | flops 943718400 | bytes 5447680 | tf_op jit(solution)/shard_map/dot_general | solution.py:38
  65.2 0.4 fusion.79
  65.6 4.5 %collective-permute-start.4 = (bf16[1,128,160]{1,2,0:T(8,128)(2,1)S(1)}, bf16[1,128,160]{1,2,0:T(8,128)(2,1)S(1)}, u32[]{:S(2)}, u32[]{:S(2)}) collective-permute-start(bf16[1,128,160]{1,2,0:T(8,128)(2,1)S(1)} %get-tuple-element.21), channel_id=1, source_target_pairs={{0,2},{2,4},{4,6},{1,3},{3,5},{5,7},{8,10},{10,12},{12,14},{9,11},... | collective-permute-start | bytes 122888 | tf_op jit(solution)/shard_map/ppermute | solution.py:17
  70.1 1.3 %collective-permute-start.5 = (bf16[1,128,160]{1,2,0:T(8,128)(2,1)S(1)}, bf16[1,128,160]{1,2,0:T(8,128)(2,1)S(1)}, u32[]{:S(2)}, u32[]{:S(2)}) collective-permute-start(bf16[1,128,160]{1,2,0:T(8,128)(2,1)S(1)} %get-tuple-element.22), channel_id=1, source_target_pairs={{2,0},{4,2},{6,4},{3,1},{5,3},{7,5},{10,8},{12,10},{14,12},{11,9},... | collective-permute-start | bytes 122888 | tf_op jit(solution)/shard_map/ppermute | solution.py:19
  71.4 1.3 %fusion.124 = f32[4,128,1440]{1,2,0:T(8,128)S(1)} fusion(bf16[640,1440,1]{0,1,2:T(8,128)(2,1)S(1)} %bitcast.99, bf16[4,128,640]{1,2,0:T(8,128)(2,1)S(1)} %bitcast.91), kind=kOutput, calls=%fused_computation.198 | convolution fusion | flops 943718400 | bytes 5447680 | tf_op jit(solution)/shard_map/dot_general | solution.py:38
  72.7 0.4 fusion.69
  73.1 6.1 %all_gather.49 = bf16[2,128,640]{1,2,0:T(8,128)(2,1)S(1)} all-gather(bf16[2,128,160]{1,2,0:T(8,128)(2,1)S(1)} %fusion.69), channel_id=1, replica_groups=mesh['groups'=2,'section'=2,'band'=4,'chan'=2] {'section','chan'}, dimensions={2}, use_global_device_ids=true | all-gather | bytes 409600 | tf_op jit(solution)/shard_map/all_gather | solution.py:104
  79.2 1.3 %collective-permute-start.11 = (bf16[1,128,640]{1,2,0:T(8,128)(2,1)S(1)}, bf16[1,128,640]{1,2,0:T(8,128)(2,1)S(1)}, u32[]{:S(2)}, u32[]{:S(2)}) collective-permute-start(bf16[1,128,640]{1,2,0:T(8,128)(2,1)S(1)} %get-tuple-element.17), channel_id=1, source_target_pairs={{2,0},{4,2},{6,4},{3,1},{5,3},{7,5},{10,8},{12,10},{14,12},{11,9},... | collective-permute-start | bytes 491528 | tf_op jit(solution)/shard_map/ppermute | solution.py:19
  80.5 5.2 %collective-permute-start.10 = (bf16[1,128,640]{1,2,0:T(8,128)(2,1)S(1)}, bf16[1,128,640]{1,2,0:T(8,128)(2,1)S(1)}, u32[]{:S(2)}, u32[]{:S(2)}) collective-permute-start(bf16[1,128,640]{1,2,0:T(8,128)(2,1)S(1)} %get-tuple-element.18), channel_id=1, source_target_pairs={{0,2},{2,4},{4,6},{1,3},{3,5},{5,7},{8,10},{10,12},{12,14},{9,11},... | collective-permute-start | bytes 491528 | tf_op jit(solution)/shard_map/ppermute | solution.py:17
  85.8 7.7 %all-gather.2 = bf16[16,128,160]{1,2,0:T(8,128)(2,1)S(1)} all-gather(bf16[4,128,160]{1,2,0:T(8,128)(2,1)S(1)} %pad_maximum_fusion.2), channel_id=4, replica_groups=mesh['groups'=2,'section'=2,'band'=4,'chan'=2] {'section','chan'}, dimensions={0}, use_global_device_ids=true | all-gather | bytes 819200 | tf_op jit(solution)/shard_map/all_gather | solution.py:64
  93.6 1.3 %fusion.122 = f32[4,128,1440]{1,2,0:T(8,128)S(1)} fusion(bf16[640,1440,1]{0,1,2:T(8,128)(2,1)S(1)} %bitcast.90, bf16[4,128,640]{1,2,0:T(8,128)(2,1)S(1)} %bitcast.94), kind=kOutput, calls=%fused_computation.196 | convolution fusion | flops 943718400 | bytes 5447680 | tf_op jit(solution)/shard_map/dot_general | solution.py:38
  95.0 1.3 %fusion.125 = f32[4,128,1440]{1,2,0:T(8,128)S(1)} fusion(bf16[640,1440,1]{0,1,2:T(8,128)(2,1)S(1)} %bitcast.89, bf16[4,128,640]{1,2,0:T(8,128)(2,1)S(1)} %constant_dynamic-update-slice_fusion), kind=kOutput, calls=%fused_computation.199 | convolution fusion | flops 943718400 | bytes 5447680 | tf_op jit(solution)/shard_map/dot_general | solution.py:38
  96.3 0.6 fusion.97
  97.0 3.9 %collective-permute-start.12 = (bf16[1,128,160]{1,2,0:T(8,128)(2,1)S(1)}, bf16[1,128,160]{1,2,0:T(8,128)(2,1)S(1)}, u32[]{:S(2)}, u32[]{:S(2)}) collective-permute-start(bf16[1,128,160]{1,2,0:T(8,128)(2,1)S(1)} %get-tuple-element.19), channel_id=1, source_target_pairs={{0,2},{2,4},{4,6},{1,3},{3,5},{5,7},{8,10},{10,12},{12,14},{9,11},... | collective-permute-start | bytes 122888 | tf_op jit(solution)/shard_map/ppermute | solution.py:17
  100.9 1.5 %collective-permute-start.13 = (bf16[1,128,160]{1,2,0:T(8,128)(2,1)S(1)}, bf16[1,128,160]{1,2,0:T(8,128)(2,1)S(1)}, u32[]{:S(2)}, u32[]{:S(2)}) collective-permute-start(bf16[1,128,160]{1,2,0:T(8,128)(2,1)S(1)} %get-tuple-element.20), channel_id=1, source_target_pairs={{2,0},{4,2},{6,4},{3,1},{5,3},{7,5},{10,8},{12,10},{14,12},{11,9},... | collective-permute-start | bytes 122888 | tf_op jit(solution)/shard_map/ppermute | solution.py:19
  102.4 1.3 %fusion.127 = f32[4,128,1440]{1,2,0:T(8,128)S(1)} fusion(bf16[640,1440,1]{0,1,2:T(8,128)(2,1)S(1)} %bitcast.88, bf16[4,128,640]{1,2,0:T(8,128)(2,1)S(1)} %constant_dynamic-update-slice_fusion), kind=kOutput, calls=%fused_computation.201 | convolution fusion | flops 943718400 | bytes 5447680 | tf_op jit(solution)/shard_map/dot_general | solution.py:38
  103.7 3.3 %collective-permute-done.13 = bf16[1,128,160]{1,2,0:T(8,128)(2,1)S(1)} collective-permute-done((bf16[1,128,160]{1,2,0:T(8,128)(2,1)S(1)}, bf16[1,128,160]{1,2,0:T(8,128)(2,1)S(1)}, u32[]{:S(2)}, u32[]{:S(2)}) %collective-permute-start.13) | collective-permute-done | bytes 40992 | tf_op jit(solution)/shard_map/ppermute | solution.py:19
  107.0 7.4 %all-gather.5 = bf16[16,128,160]{1,2,0:T(8,128)(2,1)S(1)} all-gather(bf16[4,128,160]{1,2,0:T(8,128)(2,1)S(1)} %pad_maximum_fusion.5), channel_id=7, replica_groups=mesh['groups'=2,'section'=2,'band'=4,'chan'=2] {'section','chan'}, dimensions={0}, use_global_device_ids=true | all-gather | bytes 819200 | tf_op jit(solution)/shard_map/all_gather | solution.py:64
  114.5 1.3 %fusion.126 = f32[4,128,1440]{1,2,0:T(8,128)S(1)} fusion(bf16[640,1440,1]{0,1,2:T(8,128)(2,1)S(1)} %bitcast.87, bf16[4,128,640]{1,2,0:T(8,128)(2,1)S(1)} %bitcast.93), kind=kOutput, calls=%fused_computation.200 | convolution fusion | flops 943718400 | bytes 5447680 | tf_op jit(solution)/shard_map/dot_general | solution.py:38
  115.8 1.2 %fusion.99 = bf16[2,128,160]{1,2,0:T(8,128)(2,1)} fusion(bf16[2,128,160]{1,2,0:T(8,128)(2,1)S(1)} %get-tuple-element.6, f32[4,128,1440]{1,2,0:T(8,128)S(1)} %fusion.127, f32[4,128,1440]{1,2,0:T(8,128)S(1)} %fusion.126, f32[160]{0:T(256)S(1)} %convert_element_type.126), kind=kLoop, calls=%fused_computation.168 | loop fusion | flops 860160 | bytes 7046144 | tf_op jit(solution)/shard_map/convert_element_type | solution.py:77
  (57 shorter events, 0.6 us)
Async XLA Ops:
  0.0 34.2 %copy-start = (bf16[3,3,160,640]{3,2,1,0:T(8,128)(2,1)S(1)}, bf16[3,3,160,640]{3,2,1,0:T(8,128)(2,1)}, u32[]{:S(2)}) copy-start(bf16[3,3,160,640]{3,2,1,0:T(8,128)(2,1)} %param.20) | copy-start | bytes 5529604
  1.2 25.0 %collective-permute-start = (bf16[1,128,160]{1,2,0:T(8,128)(2,1)S(1)}, bf16[1,128,160]{1,2,0:T(8,128)(2,1)S(1)}, u32[]{:S(2)}, u32[]{:S(2)}) collective-permute-start(bf16[1,128,160]{1,2,0:T(8,128)(2,1)S(1)} %get-tuple-element.27), channel_id=1, source_target_pairs={{0,2},{2,4},{4,6},{1,3},{3,5},{5,7},{8,10},{10,12},{12,14},{9,11},... | collective-permute-start | bytes 122888 | tf_op jit(solution)/shard_map/ppermute | solution.py:17
  6.1 20.0 %collective-permute-start.1 = (bf16[1,128,160]{1,2,0:T(8,128)(2,1)S(1)}, bf16[1,128,160]{1,2,0:T(8,128)(2,1)S(1)}, u32[]{:S(2)}, u32[]{:S(2)}) collective-permute-start(bf16[1,128,160]{1,2,0:T(8,128)(2,1)S(1)} %get-tuple-element.28), channel_id=1, source_target_pairs={{2,0},{4,2},{6,4},{3,1},{5,3},{7,5},{10,8},{12,10},{14,12},{11,9},... | collective-permute-start | bytes 122888 | tf_op jit(solution)/shard_map/ppermute | solution.py:19
  7.5 9.3 %collective-permute-start.6 = (bf16[1,128,160]{1,2,0:T(8,128)(2,1)S(1)}, bf16[1,128,160]{1,2,0:T(8,128)(2,1)S(1)}, u32[]{:S(2)}, u32[]{:S(2)}) collective-permute-start(bf16[1,128,160]{1,2,0:T(8,128)(2,1)S(1)} %get-tuple-element.33), channel_id=1, source_target_pairs={{0,2},{2,4},{4,6},{1,3},{3,5},{5,7},{8,10},{10,12},{12,14},{9,11},... | collective-permute-start | bytes 122888 | tf_op jit(solution)/shard_map/ppermute | solution.py:17
  12.0 4.0 %copy-start.1 = (bf16[3,3,160,1280]{3,2,1,0:T(8,128)(2,1)S(1)}, bf16[3,3,160,1280]{3,2,1,0:T(8,128)(2,1)}, u32[]{:S(2)}) copy-start(bf16[3,3,160,1280]{3,2,1,0:T(8,128)(2,1)} %param.26) | copy-start | bytes 11059204
  12.0 6.2 %collective-permute-start.7 = (bf16[1,128,160]{1,2,0:T(8,128)(2,1)S(1)}, bf16[1,128,160]{1,2,0:T(8,128)(2,1)S(1)}, u32[]{:S(2)}, u32[]{:S(2)}) collective-permute-start(bf16[1,128,160]{1,2,0:T(8,128)(2,1)S(1)} %get-tuple-element.34), channel_id=1, source_target_pairs={{2,0},{4,2},{6,4},{3,1},{5,3},{7,5},{10,8},{12,10},{14,12},{11,9},... | collective-permute-start | bytes 122888 | tf_op jit(solution)/shard_map/ppermute | solution.py:19
  16.0 0.7 copy-start.7
  16.0 0.7 copy-start.8
  16.0 0.7 copy-start.9
  16.0 0.7 copy-start.10
  16.0 0.7 copy-start.11
  16.0 0.7 copy-start.12
  34.3 1.5 %copy-start.4 = (bf16[3,3,160,640]{3,2,1,0:T(8,128)(2,1)S(1)}, bf16[3,3,160,640]{3,2,1,0:T(8,128)(2,1)}, u32[]{:S(2)}) copy-start(bf16[3,3,160,640]{3,2,1,0:T(8,128)(2,1)} %param.16) | copy-start | bytes 5529604
  35.6 1.5 %copy-start.2 = (bf16[2,128,160]{1,2,0:T(8,128)(2,1)S(1)}, bf16[2,128,160]{1,2,0:T(8,128)(2,1)}, u32[]{:S(2)}) copy-start(bf16[2,128,160]{1,2,0:T(8,128)(2,1)} %param.14) | copy-start | bytes 245764
  35.6 1.5 %copy-start.3 = (bf16[2,128,160]{1,2,0:T(8,128)(2,1)S(1)}, bf16[2,128,160]{1,2,0:T(8,128)(2,1)}, u32[]{:S(2)}) copy-start(bf16[2,128,160]{1,2,0:T(8,128)(2,1)} %param.15) | copy-start | bytes 245764
  37.7 26.2 %copy-start.5 = (bf16[3,3,160,640]{3,2,1,0:T(8,128)(2,1)S(1)}, bf16[3,3,160,640]{3,2,1,0:T(8,128)(2,1)}, u32[]{:S(2)}) copy-start(bf16[3,3,160,640]{3,2,1,0:T(8,128)(2,1)} %param.22) | copy-start | bytes 5529604
  37.8 10.8 %collective-permute-start.8 = (bf16[1,128,160]{1,2,0:T(8,128)(2,1)S(1)}, bf16[1,128,160]{1,2,0:T(8,128)(2,1)S(1)}, u32[]{:S(2)}, u32[]{:S(2)}) collective-permute-start(bf16[1,128,160]{1,2,0:T(8,128)(2,1)S(1)} %get-tuple-element.31), channel_id=1, source_target_pairs={{0,2},{2,4},{4,6},{1,3},{3,5},{5,7},{8,10},{10,12},{12,14},{9,11},... | collective-permute-start | bytes 122888 | tf_op jit(solution)/shard_map/ppermute | solution.py:17
  41.4 7.2 %collective-permute-start.9 = (bf16[1,128,160]{1,2,0:T(8,128)(2,1)S(1)}, bf16[1,128,160]{1,2,0:T(8,128)(2,1)S(1)}, u32[]{:S(2)}, u32[]{:S(2)}) collective-permute-start(bf16[1,128,160]{1,2,0:T(8,128)(2,1)S(1)} %get-tuple-element.32), channel_id=1, source_target_pairs={{2,0},{4,2},{6,4},{3,1},{5,3},{7,5},{10,8},{12,10},{14,12},{11,9},... | collective-permute-start | bytes 122888 | tf_op jit(solution)/shard_map/ppermute | solution.py:19
  42.7 13.1 %collective-permute-start.2 = (bf16[1,128,160]{1,2,0:T(8,128)(2,1)S(1)}, bf16[1,128,160]{1,2,0:T(8,128)(2,1)S(1)}, u32[]{:S(2)}, u32[]{:S(2)}) collective-permute-start(bf16[1,128,160]{1,2,0:T(8,128)(2,1)S(1)} %get-tuple-element.23), channel_id=1, source_target_pairs={{0,2},{2,4},{4,6},{1,3},{3,5},{5,7},{8,10},{10,12},{12,14},{9,11},... | collective-permute-start | bytes 122888 | tf_op jit(solution)/shard_map/ppermute | solution.py:17
  47.3 8.6 %collective-permute-start.3 = (bf16[1,128,160]{1,2,0:T(8,128)(2,1)S(1)}, bf16[1,128,160]{1,2,0:T(8,128)(2,1)S(1)}, u32[]{:S(2)}, u32[]{:S(2)}) collective-permute-start(bf16[1,128,160]{1,2,0:T(8,128)(2,1)S(1)} %get-tuple-element.24), channel_id=1, source_target_pairs={{2,0},{4,2},{6,4},{3,1},{5,3},{7,5},{10,8},{12,10},{14,12},{11,9},... | collective-permute-start | bytes 122888 | tf_op jit(solution)/shard_map/ppermute | solution.py:19
  65.2 6.2 %copy-start.6 = (bf16[3,3,160,640]{3,2,1,0:T(8,128)(2,1)S(1)}, bf16[3,3,160,640]{3,2,1,0:T(8,128)(2,1)}, u32[]{:S(2)}) copy-start(bf16[3,3,160,640]{3,2,1,0:T(8,128)(2,1)} %param.18) | copy-start | bytes 5529604
  65.6 20.1 %collective-permute-start.4 = (bf16[1,128,160]{1,2,0:T(8,128)(2,1)S(1)}, bf16[1,128,160]{1,2,0:T(8,128)(2,1)S(1)}, u32[]{:S(2)}, u32[]{:S(2)}) collective-permute-start(bf16[1,128,160]{1,2,0:T(8,128)(2,1)S(1)} %get-tuple-element.21), channel_id=1, source_target_pairs={{0,2},{2,4},{4,6},{1,3},{3,5},{5,7},{8,10},{10,12},{12,14},{9,11},... | collective-permute-start | bytes 122888 | tf_op jit(solution)/shard_map/ppermute | solution.py:17
  70.1 15.6 %collective-permute-start.5 = (bf16[1,128,160]{1,2,0:T(8,128)(2,1)S(1)}, bf16[1,128,160]{1,2,0:T(8,128)(2,1)S(1)}, u32[]{:S(2)}, u32[]{:S(2)}) collective-permute-start(bf16[1,128,160]{1,2,0:T(8,128)(2,1)S(1)} %get-tuple-element.22), channel_id=1, source_target_pairs={{2,0},{4,2},{6,4},{3,1},{5,3},{7,5},{10,8},{12,10},{14,12},{11,9},... | collective-permute-start | bytes 122888 | tf_op jit(solution)/shard_map/ppermute | solution.py:19
  79.2 15.7 %collective-permute-start.11 = (bf16[1,128,640]{1,2,0:T(8,128)(2,1)S(1)}, bf16[1,128,640]{1,2,0:T(8,128)(2,1)S(1)}, u32[]{:S(2)}, u32[]{:S(2)}) collective-permute-start(bf16[1,128,640]{1,2,0:T(8,128)(2,1)S(1)} %get-tuple-element.17), channel_id=1, source_target_pairs={{2,0},{4,2},{6,4},{3,1},{5,3},{7,5},{10,8},{12,10},{14,12},{11,9},... | collective-permute-start | bytes 491528 | tf_op jit(solution)/shard_map/ppermute | solution.py:19
  80.5 14.4 %collective-permute-start.10 = (bf16[1,128,640]{1,2,0:T(8,128)(2,1)S(1)}, bf16[1,128,640]{1,2,0:T(8,128)(2,1)S(1)}, u32[]{:S(2)}, u32[]{:S(2)}) collective-permute-start(bf16[1,128,640]{1,2,0:T(8,128)(2,1)S(1)} %get-tuple-element.18), channel_id=1, source_target_pairs={{0,2},{2,4},{4,6},{1,3},{3,5},{5,7},{8,10},{10,12},{12,14},{9,11},... | collective-permute-start | bytes 491528 | tf_op jit(solution)/shard_map/ppermute | solution.py:17
  97.0 6.7 %collective-permute-start.12 = (bf16[1,128,160]{1,2,0:T(8,128)(2,1)S(1)}, bf16[1,128,160]{1,2,0:T(8,128)(2,1)S(1)}, u32[]{:S(2)}, u32[]{:S(2)}) collective-permute-start(bf16[1,128,160]{1,2,0:T(8,128)(2,1)S(1)} %get-tuple-element.19), channel_id=1, source_target_pairs={{0,2},{2,4},{4,6},{1,3},{3,5},{5,7},{8,10},{10,12},{12,14},{9,11},... | collective-permute-start | bytes 122888 | tf_op jit(solution)/shard_map/ppermute | solution.py:17
  100.9 6.1 %collective-permute-start.13 = (bf16[1,128,160]{1,2,0:T(8,128)(2,1)S(1)}, bf16[1,128,160]{1,2,0:T(8,128)(2,1)S(1)}, u32[]{:S(2)}, u32[]{:S(2)}) collective-permute-start(bf16[1,128,160]{1,2,0:T(8,128)(2,1)S(1)} %get-tuple-element.20), channel_id=1, source_target_pairs={{2,0},{4,2},{6,4},{3,1},{5,3},{7,5},{10,8},{12,10},{14,12},{11,9},... | collective-permute-start | bytes 122888 | tf_op jit(solution)/shard_map/ppermute | solution.py:19
